TPU v7x, 32 devices: a whole 2x2x4 slice. The times are simulated.
32 devices in a mesh: groups: 2 (over x), tensor: 8 (over z, y), dp: 2 (over core).
Axes of the slice: x: 2, y: 2, z: 4, core: 2. Of those that a mesh axis runs over, the one named last changes fastest.
Arguments:
- inputs: bfloat16 [4, 256, 16384], P(('groups', 'dp'), None, 'tensor'), parts along dimension 0, may hold values from -6 to 6
- cross_w: bfloat16 [16384, 16384], P('dp', 'tensor'), may hold values from -0.046875 to 0.046875
- cross_b: float32 [16384], P('tensor'), may hold values from -3 to 3
- mix_weight: bfloat16 [128, 512], replicated, may hold values from -0.5 to 0.5
- mix_bias: float32 [512], replicated, may hold values from -3 to 3
- out_weight: bfloat16 [512, 128], replicated, may hold values from -0.25 to 0.25
- cotangent: bfloat16 [4, 256, 16384], P(('groups', 'dp'), 'tensor'), parts along dimension 0, may hold values from -12 to 12
Outputs:
- compressed: bfloat16 [4, 256, 16384], P(('groups', 'dp'), 'tensor'), parts along dimension 0
- grad_inputs: bfloat16 [4, 256, 16384], P(('groups', 'dp'), None, 'tensor'), parts along dimension 0
- grad_mix: float32 [256, 512], P('groups'), parts along dimension 0
- grad_mix_bias: float32 [1024], P('groups'), parts along dimension 0
- grad_out: float32 [1024, 128], P('groups'), parts along dimension 0
There are 2 independent parts, one for each index of `groups`. A program takes and returns all parts, laid end to end along the dimension named above; an argument that names none is the same for every part. Nothing has to cross between parts.
All inputs are finite; a program needn't handle non-finite values.
Results may differ from a plain program's by a relative error of at most 0.019.
Values may be sent and summed in bfloat16 or wider, within the bound.
No kernel may reach another device: no remote copies, remote signals or barrier semaphores. Data moves between devices by JAX's collectives and lax.ppermute only.
A program may use at most 256 MiB of HBM per device.

v0:
```python
import jax
import jax.numpy as jnp
from jax import lax
from jax.sharding import PartitionSpec as P

F = 128
E = 128
K = 128


def shards(inputs, cross_w, cross_b, mix_weight, mix_bias, out_weight, cotangent):
    local_rows = inputs[0]
    dp_count = lax.axis_size("dp")
    full_rows = lax.all_gather(local_rows, "tensor", axis=1, tiled=True)
    linear = jnp.dot(
        full_rows,
        lax.all_gather(cross_w, "dp", axis=0, tiled=True),
        preferred_element_type=jnp.float32,
    )
    linear = linear + cross_b
    base_rows = local_rows.astype(jnp.float32)
    crossed = (base_rows * linear + base_rows).astype(jnp.bfloat16)
    owned = lax.all_to_all(crossed, "tensor", split_axis=0, concat_axis=1, tiled=True)
    owned_count = owned.shape[0]
    grid_rows = owned.reshape(owned_count, F, E)
    gram_rows = (
        jnp.einsum("bfe,bge->bfg", grid_rows, grid_rows, preferred_element_type=jnp.float32) / E
    ).astype(jnp.bfloat16)
    pre_act = (
        jnp.einsum("bfg,gh->bfh", gram_rows, mix_weight, preferred_element_type=jnp.float32)
        + mix_bias
    )
    sigmoid_pre = jax.nn.sigmoid(pre_act)
    hidden = (pre_act * sigmoid_pre).astype(jnp.bfloat16)
    compressed = jnp.einsum(
        "bfh,hk->bfk", hidden, out_weight, preferred_element_type=jnp.float32
    ).astype(jnp.bfloat16)
    upstream = cotangent[0].reshape(owned_count, F, K)
    d_hidden = jnp.einsum("bfk,hk->bfh", upstream, out_weight, preferred_element_type=jnp.float32)
    out_term = jnp.einsum("bfh,bfk->hk", hidden, upstream, preferred_element_type=jnp.float32)
    d_pre = (d_hidden * sigmoid_pre * (1.0 + pre_act * (1.0 - sigmoid_pre))).astype(jnp.bfloat16)
    mix_term = jnp.einsum("bfg,bfh->gh", gram_rows, d_pre, preferred_element_type=jnp.float32)
    bias_term = jnp.sum(d_pre.astype(jnp.float32), axis=(0, 1))
    mix_sum, bias_sum, out_sum = (
        lax.psum(mix_term.astype(jnp.bfloat16), ("tensor", "dp")).astype(jnp.float32),
        lax.psum(bias_term.astype(jnp.bfloat16), ("tensor", "dp")).astype(jnp.float32),
        lax.psum(out_term.astype(jnp.bfloat16), ("tensor", "dp")).astype(jnp.float32),
    )
    row_total = owned_count * lax.axis_size("tensor") * dp_count
    d_gram = jnp.einsum("bfh,gh->bfg", d_pre, mix_weight, preferred_element_type=jnp.float32)
    grid_wide = grid_rows.astype(jnp.float32)
    d_grid = jnp.einsum("bfg,bge->bfe", d_gram + jnp.swapaxes(d_gram, 1, 2), grid_wide) / E
    d_owned = d_grid.astype(jnp.bfloat16).reshape(owned_count, F * E)
    d_crossed = lax.all_to_all(d_owned, "tensor", split_axis=1, concat_axis=0, tiled=True)
    d_crossed_wide = d_crossed.astype(jnp.float32)
    d_linear = (d_crossed_wide * base_rows).astype(jnp.bfloat16)
    contract = (((1,), (1,)), ((), ()))
    back_terms = lax.dot_general(
        d_linear,
        lax.all_gather(cross_w, "dp", axis=0, tiled=True),
        contract,
        preferred_element_type=jnp.float32,
    )
    back_sum = lax.psum_scatter(
        back_terms.astype(jnp.bfloat16), "tensor", scatter_dimension=1, tiled=True
    ).astype(jnp.float32)
    grad_inputs = (d_crossed_wide * (linear + 1.0) + back_sum).astype(jnp.bfloat16)
    return (
        compressed.reshape(1, owned_count, F * K),
        grad_inputs[None],
        mix_sum / row_total,
        bias_sum / row_total,
        out_sum / row_total,
    )


def solution(mesh):
    return jax.shard_map(
        shards,
        mesh=mesh,
        in_specs=(
            P(("groups", "dp"), None, "tensor"),
            P("dp", "tensor"),
            P("tensor"),
            P(),
            P(),
            P(),
            P(("groups", "dp"), "tensor", None),
        ),
        out_specs=(
            P(("groups", "dp"), "tensor", None),
            P(("groups", "dp"), None, "tensor"),
            P("groups", None),
            P("groups"),
            P("groups", None),
        ),
        check_vma=False,
    )
```

profile of v0, /device:TPU:0, one launch (start us, length us, event | category | flops | bytes accessed | tf_op | source)
XLA Modules:
  0.0 582.4 jit_solution(2011968667886465584)
XLA Ops:
  7.2 0.0 copy-start
  7.2 0.0 all-gather.6.cloned.1.call-start
  7.2 0.7 all-gather.6.cloned.1.call-update
  7.9 0.0 copy-start.2
  7.9 0.0 copy-start.11
  7.9 0.0 all-gather.4.cloned.1.call-start
  8.0 0.7 all-gather.4.cloned.1.call-update
  8.7 0.0 copy-start.7
  8.7 129.2 %all-gather.6.cloned.1.call-done = bf16[1,256,16384]{2,1,0:T(8,128)(2,1)} async-done(((bf16[1,256,2048]{2,1,0:T(8,128)(2,1)}), bf16[1,256,16384]{2,1,0:T(8,128)(2,1)}) %all-gather.6.cloned.1.call-update) | async-done | bytes 8388624 | tf_op jit(solution)/shard_map/all_gather | solution.py:14
  137.9 94.9 %all-gather.4.cloned.1.call-done = bf16[16384,2048]{1,0:T(8,128)(2,1)} async-done(((bf16[8192,2048]{1,0:T(8,128)(2,1)}), bf16[16384,2048]{1,0:T(8,128)(2,1)}) %all-gather.4.cloned.1.call-update) | async-done | bytes 67108880 | tf_op jit(solution)/shard_map/all_gather | solution.py:17
  232.7 0.0 copy-done.2
  232.7 0.0 copy-done.11
  232.7 29.4 %fusion.5 = (bf16[256,2048]{1,0:T(8,128)(2,1)}, f32[256,2048]{1,0:T(8,128)}) fusion(bf16[1,256,2048]{2,1,0:T(8,128)(2,1)S(1)} %copy-done.2, f32[2048]{0:T(1024)S(1)} %copy-done.11, bf16[16384,2048]{1,0:T(8,128)(2,1)} %all-gather.4.cloned.1.call-done, bf16[1,256,16384]{2,1,0:T(8,128)(2,1)} %all-gather.6.cloned.1.call-done), kind=kOutput, calls=%fused_computation.10 | convolution fusion | flops 17182490624 | bytes 79699968 | tf_op jit(solution)/shard_map/dot_general | solution.py:15
  262.2 5.8 all-to-all-start
  267.9 0.0 copy-done.7
  267.9 0.2 copy.19
  268.2 0.0 copy-start.8
  268.2 0.0 copy-start.12
  268.2 26.0 %all-to-all-done = bf16[8,32,2048]{2,1,0:T(8,128)(2,1)S(1)} async-done(((bf16[8,32,2048]{2,1,0:T(8,128)(2,1)}), bf16[8,32,2048]{2,1,0:T(8,128)(2,1)S(1)}, u32[]{:S(2)}, u32[]{:S(2)}) %all-to-all-start) | async-done | bytes 1048608 | tf_op jit(solution)/shard_map/all_to_all | solution.py:23
  294.2 0.6 copy.12
  294.7 0.5 reshape.29
  295.3 0.8 multiply_convert_fusion.3
  296.1 0.0 copy-done
  296.1 0.0 copy-done.12
  296.1 0.0 copy-start.5
  296.2 0.0 copy-start.10
  296.2 3.9 multiply_convert_fusion.1
  300.1 0.0 copy-done.5
  300.1 0.0 copy-done.8
  300.1 0.0 copy-done.10
  300.1 3.7 fusion.18
  303.8 0.0 copy-start.1
  303.8 2.0 copy-done.1
  305.7 1.2 fusion.14
  307.0 1.8 copy.13
  308.8 3.0 multiply_convert_fusion.2
  311.8 0.0 copy-start.6
  311.8 1.6 all_to_all.25
  313.4 1.5 copy.14
  315.0 0.0 copy-start.9
  315.0 3.8 all-to-all-start.1
  318.8 0.2 all-reduce.3.cloned.1.call-start
  319.0 0.0 copy-done.6
  319.0 0.0 copy-start.4
  319.0 3.7 fusion.10
  322.8 0.0 copy-done.9
  322.8 0.0 copy-done.4
  322.8 2.0 fusion.11
  324.7 0.0 all-reduce.3.cloned.1.call-update
  324.8 0.0 reduce-scatter.2.cloned.1.call-start
  324.8 20.7 %all-to-all-done.1 = bf16[32,8,2048]{2,0,1:T(8,128)(2,1)S(1)} async-done(((bf16[32,8,2048]{2,0,1:T(8,128)(2,1)}), bf16[32,8,2048]{2,0,1:T(8,128)(2,1)S(1)}, u32[]{:S(2)}, u32[]{:S(2)}) %all-to-all-start.1) | async-done | bytes 1048608 | tf_op jit(solution)/shard_map/all_to_all | solution.py:54
  345.5 0.0 copy-done.3
  345.5 0.4 fusion.6
  345.9 30.1 %convolution_convert_fusion = bf16[256,16384]{1,0:T(8,128)(2,1)} fusion(bf16[256,2048]{1,0:T(8,128)(2,1)S(1)} %fusion.6, bf16[16384,2048]{1,0:T(8,128)(2,1)} %all-gather.4.cloned.1.call-done), kind=kOutput, calls=%fused_computation | convolution fusion | flops 17184063488 | bytes 76546048 | tf_op jit(solution)/shard_map/dot_general | solution.py:58
  376.0 0.0 reduce-scatter.2.cloned.1.call-update
  376.0 3.4 convolution_convert_fusion.1
  379.4 1.3 reshape.30
  380.7 31.5 %psum.22 = bf16[512]{0:T(512)(128)(2,1)S(1)} all-reduce(bf16[512]{0:T(512)(128)(2,1)S(1)} %get-tuple-element.11), channel_id=1, replica_groups=mesh['groups'=2,'tensor'=8,'dp'=2] {'tensor','dp'}, use_global_device_ids=true, to_apply=%region_3.0 | all-reduce | flops 512 | bytes 2048 | tf_op jit(solution)/shard_map/psum | solution.py:46
  412.2 0.6 convert_multiply_fusion.4
  412.8 6.3 %all-reduce.3.cloned.1.call-done = (bf16[128,512]{1,0:T(8,128)(2,1)}, bf16[512,128]{1,0:T(8,128)(2,1)}) async-done(((bf16[128,512]{1,0:T(8,128)(2,1)}, bf16[512,128]{1,0:T(8,128)(2,1)}), (bf16[128,512]{1,0:T(8,128)(2,1)}, bf16[512,128]{1,0:T(8,128)(2,1)})) %all-reduce.3.cloned.1.call-update) | async-done | bytes 262160 | tf_op jit(solution)/shard_map/psum | solution.py:45
  419.1 1.6 convert_multiply_fusion.3
  420.8 1.6 convert_multiply_fusion.2
  422.4 150.2 %reduce-scatter.2.cloned.1.call-done = bf16[256,2048]{1,0:T(8,128)(2,1)} async-done(((bf16[256,16384]{1,0:T(8,128)(2,1)}), bf16[256,2048]{1,0:T(8,128)(2,1)}) %reduce-scatter.2.cloned.1.call-update) | async-done | bytes 1048592 | tf_op jit(solution)/shard_map/reduce_scatter | solution.py:64
  572.5 3.3 fusion.8
  (1 shorter events, 0.0 us)
Async XLA Ops:
  7.2 289.0 %copy-start = (bf16[128,512]{1,0:T(8,128)(2,1)S(1)}, bf16[128,512]{1,0:T(8,128)(2,1)}, u32[]{:S(2)}) copy-start(bf16[128,512]{1,0:T(8,128)(2,1)} %param.10) | copy-start | bytes 393220
  7.2 130.7 %all-gather.6.cloned.1.call-start = ((), (), s32[]{:S(2)}) async-start(), calls=%async_computation.5 | async-start | bytes 9437184 | tf_op jit(solution)/shard_map/all_gather | solution.py:14
  7.9 224.8 %copy-start.2 = (bf16[1,256,2048]{2,1,0:T(8,128)(2,1)S(1)}, bf16[1,256,2048]{2,1,0:T(8,128)(2,1)}, u32[]{:S(2)}) copy-start(bf16[1,256,2048]{2,1,0:T(8,128)(2,1)} %param.7) | copy-start | bytes 3145732
  7.9 224.8 %copy-start.11 = (f32[2048]{0:T(1024)S(1)}, f32[2048]{0:T(1024)}, u32[]{:S(2)}) copy-start(f32[2048]{0:T(1024)} %param.9) | copy-start | bytes 24580
  7.9 224.8 %all-gather.4.cloned.1.call-start = ((), (), s32[]{:S(2)}) async-start(), calls=%async_computation.3 | async-start | bytes 100663296 | tf_op jit(solution)/shard_map/all_gather | solution.py:17
  8.7 259.2 %copy-start.7 = (bf16[1,32,16384]{2,1,0:T(8,128)(2,1)S(1)}, bf16[1,32,16384]{2,1,0:T(8,128)(2,1)}, u32[]{:S(2)}) copy-start(bf16[1,32,16384]{2,1,0:T(8,128)(2,1)} %param.13) | copy-start | bytes 3145732
  262.2 32.0 %all-to-all-start = ((bf16[8,32,2048]{2,1,0:T(8,128)(2,1)}), bf16[8,32,2048]{2,1,0:T(8,128)(2,1)S(1)}, u32[]{:S(2)}, u32[]{:S(2)}) async-start(bf16[8,32,2048]{2,1,0:T(8,128)(2,1)} %bitcast.2), calls=%async_computation | async-start | bytes 2097152 | tf_op jit(solution)/shard_map/all_to_all | solution.py:23
  268.2 31.9 %copy-start.8 = (bf16[4,8,128,128]{3,2,1,0:T(8,128)(2,1)}, bf16[4,8,128,128]{3,2,1,0:T(8,128)(2,1)S(1)}, u32[]{:S(2)}) copy-start(bf16[4,8,128,128]{3,2,1,0:T(8,128)(2,1)S(1)} %copy.19) | copy-start | bytes 3145732
  268.2 27.9 %copy-start.12 = (f32[512]{0:T(512)S(1)}, f32[512]{0:T(512)}, u32[]{:S(2)}) copy-start(f32[512]{0:T(512)} %param.11) | copy-start | bytes 6148
  296.1 3.9 copy-start.5
  296.2 3.9 copy-start.10
  303.8 2.0 copy-start.1
  311.8 7.2 %copy-start.6 = (bf16[32,128,128]{2,1,0:T(8,128)(2,1)S(1)}, bf16[32,128,128]{2,1,0:T(8,128)(2,1)}, u32[]{:S(2)}) copy-start(bf16[32,128,128]{2,1,0:T(8,128)(2,1)} %copy-done.5) | copy-start | bytes 3145732
  315.0 7.8 %copy-start.9 = (bf16[4,8,128,128]{3,2,1,0:T(8,128)(2,1)S(1)}, bf16[4,8,128,128]{3,2,1,0:T(8,128)(2,1)}, u32[]{:S(2)}) copy-start(bf16[4,8,128,128]{3,2,1,0:T(8,128)(2,1)} %copy-done.8) | copy-start | bytes 3145732
  315.0 30.5 %all-to-all-start.1 = ((bf16[32,8,2048]{2,0,1:T(8,128)(2,1)}), bf16[32,8,2048]{2,0,1:T(8,128)(2,1)S(1)}, u32[]{:S(2)}, u32[]{:S(2)}) async-start(bf16[32,8,2048]{2,0,1:T(8,128)(2,1)} %copy.14), calls=%async_computation.1 | async-start | bytes 2097152 | tf_op jit(solution)/shard_map/all_to_all | solution.py:54
  318.8 100.4 %all-reduce.3.cloned.1.call-start = ((), (), s32[]{:S(2)}) async-start(), calls=%async_computation.6 | async-start | bytes 524288 | tf_op jit(solution)/shard_map/psum | solution.py:45
  319.0 3.8 copy-start.4
  322.8 22.8 %copy-start.3 = (bf16[1,256,2048]{2,1,0:T(8,128)(2,1)S(1)}, bf16[1,256,2048]{2,1,0:T(8,128)(2,1)}, u32[]{:S(2)}) copy-start(bf16[1,256,2048]{2,1,0:T(8,128)(2,1)} %param.7) | copy-start | bytes 3145732
  324.8 247.8 %reduce-scatter.2.cloned.1.call-start = ((), (), s32[]{:S(2)}) async-start(), calls=%async_computation.4 | async-start | bytes 9437184 | tf_op jit(solution)/shard_map/reduce_scatter | solution.py:64
Sparse Core Ops, SparseCore 0:
  10.2 127.6 all-gather.5
  139.4 93.2 all-gather.3
  324.9 94.2 all-reduce.2
  422.6 149.8 reduce-scatter.1
where the time goes:
time: 583 us; the launch traced here: 582 us
  waiting for transfers between devices  429 us (74%)
  matrix products  81.3 us (14%)
  blocking collectives  31.5 us (5%)
  between operations  13.9 us (2%)
  starting transfers between devices  9.88 us (2%)
  local copies, waits for them, and re-layouts  9.63 us (2%)
  other arithmetic  7.58 us (1%)
    reduce_scatter x1, waiting for transfers between devices, shards(): lax.psum_scatter(back_terms.astype(jnp.bfloat16), 'tensor', scatter_dimen...  150 us
    all_gather x1, waiting for transfers between devices, shards(): full_rows = lax.all_gather(local_rows, 'tensor', axis=1, tiled=True)  129 us
    all_gather x1, waiting for transfers between devices, shards(): lax.all_gather(cross_w, 'dp', axis=0, tiled=True)  94.9 us
    psum x1, blocking collectives, shards(): lax.psum(bias_term.astype(jnp.bfloat16), ('tensor', 'dp'))  31.5 us
    dot_general x1, matrix products, shards(): lax.dot_general(d_linear, lax.all_gather(cross_w, 'dp', axis=0, tiled=Tru...  30.1 us
    dot_general x1, matrix products, shards(): jnp.dot(full_rows, lax.all_gather(cross_w, 'dp', axis=0, tiled=True), pre...  29.4 us
    all_to_all x1, waiting for transfers between devices, shards(): lax.all_to_all(crossed, 'tensor', split_axis=0, concat_axis=1, tiled=True)  26 us
    all_to_all x1, waiting for transfers between devices, shards(): lax.all_to_all(d_owned, 'tensor', split_axis=1, concat_axis=0, tiled=True)  20.7 us
  transfers between devices with their start and end apart: 6, of which 6 were waited for; matrix products, arithmetic and copies ran while one was open for 8% of the time, Pallas kernels for 0%

commit v1 on v0

--- a/solution.py
+++ b/solution.py
@@ -11,7 +11,14 @@
 def shards(inputs, cross_w, cross_b, mix_weight, mix_bias, out_weight, cotangent):
     local_rows = inputs[0]
     dp_count = lax.axis_size("dp")
-    full_rows = lax.all_gather(local_rows, "tensor", axis=1, tiled=True)
+    ring = [local_rows]
+    for hop in range(7):
+        ring.append(lax.ppermute(ring[-1], "tensor", [(dev, (dev + 1) % 8) for dev in range(8)]))
+    full_rows = jnp.roll(
+        jnp.concatenate(ring[::-1], axis=1),
+        (lax.axis_index("tensor") + 1) * ring[0].shape[1],
+        axis=1,
+    )
     linear = jnp.dot(
         full_rows,
         lax.all_gather(cross_w, "dp", axis=0, tiled=True),

time: 583 us -> 554 us (0.950)
  waiting for transfers between devices: 429 us -> 370 us
  local copies, waits for them, and re-layouts: 9.63 us -> 37.8 us
    ppermute x0 -> x7, waiting for transfers between devices: none -> 175 us  [shards(): lax.ppermute(ring[-1], 'tensor', [(dev, (dev + 1) % 8) for dev in range(8)])]
    all_gather x1 -> x0, waiting for transfers between devices: 129 us -> none  [shards(): full_rows = lax.all_gather(local_rows, 'tensor', axis=1, tiled=True)]
    all_gather x1, waiting for transfers between devices: 94.9 us -> 0.01 us  [shards(): lax.all_gather(cross_w, 'dp', axis=0, tiled=True)]
    unnamed x27 -> x50, local copies, waits for them, and re-layouts: 2.28 us -> 29.3 us
    all_to_all x1, waiting for transfers between devices: 26 us -> 19.4 us  [shards(): lax.all_to_all(crossed, 'tensor', split_axis=0, concat_axis=1, tiled=True)]
  transfers between devices with their start and end apart: 6 -> 12, of which waited for: 6 -> 11; matrix products, arithmetic and copies ran while one was open for 8% -> 13% of each run, Pallas kernels for 0% -> 0%
where the time goes in v1:
time: 554 us; the launch traced here: 553 us
  waiting for transfers between devices  370 us (67%)
  matrix products  83.8 us (15%)
  local copies, waits for them, and re-layouts  37.8 us (7%)
  blocking collectives  29.6 us (5%)
  between operations  13.9 us (3%)
  starting transfers between devices  10.8 us (2%)
  other arithmetic  7.58 us (1%)
    ppermute x7, waiting for transfers between devices, shards(): lax.ppermute(ring[-1], 'tensor', [(dev, (dev + 1) % 8) for dev in range(8)])  175 us
    reduce_scatter x1, waiting for transfers between devices, shards(): lax.psum_scatter(back_terms.astype(jnp.bfloat16), 'tensor', scatter_dimen...  150 us
    dot_general x1, matrix products, shards(): lax.dot_general(d_linear, lax.all_gather(cross_w, 'dp', axis=0, tiled=Tru...  30.1 us
    psum x1, blocking collectives, shards(): lax.psum(bias_term.astype(jnp.bfloat16), ('tensor', 'dp'))  29.6 us
    dot_general x1, matrix products, shards(): jnp.dot(full_rows, lax.all_gather(cross_w, 'dp', axis=0, tiled=True), pre...  29.5 us
    unnamed x50, local copies, waits for them, and re-layouts  29.3 us
    all_to_all x1, waiting for transfers between devices, shards(): lax.all_to_all(crossed, 'tensor', split_axis=0, concat_axis=1, tiled=True)  19.4 us
    all_to_all x1, waiting for transfers between devices, shards(): lax.all_to_all(d_owned, 'tensor', split_axis=1, concat_axis=0, tiled=True)  15.2 us
  transfers between devices with their start and end apart: 12, of which 11 were waited for; matrix products, arithmetic and copies ran while one was open for 13% of the time, Pallas kernels for 0%

profile of v1, /device:TPU:0, one launch (start us, length us, event | category | flops | bytes accessed | tf_op | source)
XLA Modules:
  0.0 553.1 jit_solution(16784198843016085013)
XLA Ops:
  7.2 0.0 all-gather.2.cloned.1.call-start
  7.2 0.7 all-gather.2.cloned.1.call-update
  7.9 0.5 copy-done.2
  8.4 3.0 collective-permute-start
  11.4 26.2 %collective-permute-done = bf16[256,2048]{1,0:T(8,128)(2,1)S(1)} collective-permute-done((bf16[256,2048]{1,0:T(8,128)(2,1)S(1)}, bf16[256,2048]{1,0:T(8,128)(2,1)S(1)}, u32[]{:S(2)}, u32[]{:S(2)}) %collective-permute-start) | collective-permute-done | bytes 1048608 | tf_op jit(solution)/shard_map/ppermute | solution.py:16
  37.6 27.0 %collective-permute-done.1 = bf16[256,2048]{1,0:T(8,128)(2,1)S(1)} collective-permute-done((bf16[256,2048]{1,0:T(8,128)(2,1)S(1)}, bf16[256,2048]{1,0:T(8,128)(2,1)S(1)}, u32[]{:S(2)}, u32[]{:S(2)}) %collective-permute-start.1) | collective-permute-done | bytes 1048608 | tf_op jit(solution)/shard_map/ppermute | solution.py:16
  64.7 26.1 %collective-permute-done.2 = bf16[256,2048]{1,0:T(8,128)(2,1)S(1)} collective-permute-done((bf16[256,2048]{1,0:T(8,128)(2,1)S(1)}, bf16[256,2048]{1,0:T(8,128)(2,1)S(1)}, u32[]{:S(2)}, u32[]{:S(2)}) %collective-permute-start.2) | collective-permute-done | bytes 1048608 | tf_op jit(solution)/shard_map/ppermute | solution.py:16
  90.8 1.0 copy-done.4
  91.7 25.2 %collective-permute-done.3 = bf16[256,2048]{1,0:T(8,128)(2,1)S(1)} collective-permute-done((bf16[256,2048]{1,0:T(8,128)(2,1)S(1)}, bf16[256,2048]{1,0:T(8,128)(2,1)S(1)}, u32[]{:S(2)}, u32[]{:S(2)}) %collective-permute-start.3) | collective-permute-done | bytes 1048608 | tf_op jit(solution)/shard_map/ppermute | solution.py:16
  116.9 1.0 copy-done.6
  117.9 24.3 %collective-permute-done.4 = bf16[256,2048]{1,0:T(8,128)(2,1)S(1)} collective-permute-done((bf16[256,2048]{1,0:T(8,128)(2,1)S(1)}, bf16[256,2048]{1,0:T(8,128)(2,1)S(1)}, u32[]{:S(2)}, u32[]{:S(2)}) %collective-permute-start.4) | collective-permute-done | bytes 1048608 | tf_op jit(solution)/shard_map/ppermute | solution.py:16
  142.2 1.0 copy-done.8
  143.1 23.5 %collective-permute-done.5 = bf16[256,2048]{1,0:T(8,128)(2,1)} collective-permute-done((bf16[256,2048]{1,0:T(8,128)(2,1)S(1)}, bf16[256,2048]{1,0:T(8,128)(2,1)}, u32[]{:S(2)}, u32[]{:S(2)}) %collective-permute-start.5) | collective-permute-done | bytes 1048608 | tf_op jit(solution)/shard_map/ppermute | solution.py:16
  166.6 22.7 %collective-permute-done.6 = bf16[256,2048]{1,0:T(8,128)(2,1)} collective-permute-done((bf16[256,2048]{1,0:T(8,128)(2,1)}, bf16[256,2048]{1,0:T(8,128)(2,1)}, u32[]{:S(2)}, u32[]{:S(2)}) %collective-permute-start.6) | collective-permute-done | bytes 1048608 | tf_op jit(solution)/shard_map/ppermute | solution.py:16
  189.4 2.3 constant_dynamic-update-slice_fusion.15
  191.7 2.3 constant_dynamic-update-slice_fusion.14
  194.0 2.4 constant_dynamic-update-slice_fusion.13
  196.4 2.4 constant_dynamic-update-slice_fusion.12
  198.8 1.1 constant_dynamic-update-slice_fusion.11
  199.8 1.0 constant_dynamic-update-slice_fusion.10
  200.9 1.1 constant_dynamic-update-slice_fusion.9
  201.9 1.1 constant_dynamic-update-slice_fusion.8
  203.0 2.4 constant_dynamic-update-slice_fusion.7
  205.3 2.3 constant_dynamic-update-slice_fusion.6
  207.7 1.1 constant_dynamic-update-slice_fusion.5
  208.8 1.0 constant_dynamic-update-slice_fusion.4
  209.8 1.1 constant_dynamic-update-slice_fusion.3
  210.9 1.1 constant_dynamic-update-slice_fusion.2
  211.9 1.0 constant_dynamic-update-slice_fusion.1
  213.0 1.0 constant_dynamic-update-slice_fusion
  214.0 29.5 %fusion.6 = (bf16[256,2048]{1,0:T(8,128)(2,1)}, f32[256,2048]{1,0:T(8,128)}) fusion(bf16[1,256,2048]{2,1,0:T(8,128)(2,1)S(1)} %copy-done.2, f32[2048]{0:T(1024)S(1)} %copy-done.15, bf16[16384,2048]{1,0:T(8,128)(2,1)} %all-gather.2.cloned.1.call-done, bf16[256,32768]{1,0:T(8,128)(2,1)} %constant_dynamic-update-slice_fusion, s32[]{:T(128)S(6)} %select_n.14), kind=kOutput, calls=%fused_computation.10 | convolution fusion | flops 17182490624 | bytes 79699968 | tf_op jit(solution)/shard_map/dot_general | solution.py:22
  243.6 3.9 all-to-all-start
  247.4 0.2 copy.19
  247.7 19.4 %all-to-all-done = bf16[8,32,2048]{2,1,0:T(8,128)(2,1)S(1)} async-done(((bf16[8,32,2048]{2,1,0:T(8,128)(2,1)}), bf16[8,32,2048]{2,1,0:T(8,128)(2,1)S(1)}, u32[]{:S(2)}, u32[]{:S(2)}) %all-to-all-start) | async-done | bytes 1048608 | tf_op jit(solution)/shard_map/all_to_all | solution.py:30
  267.1 0.6 copy.12
  267.7 0.5 reshape.29
  268.3 0.8 multiply_convert_fusion.3
  269.2 3.9 multiply_convert_fusion.1
  273.1 3.7 fusion.19
  276.8 2.0 copy-done.1
  278.7 1.3 fusion.14
  280.0 1.8 copy.13
  281.8 3.0 multiply_convert_fusion.2
  284.9 1.7 all_to_all.25
  286.5 1.5 copy.14
  288.1 3.6 all-to-all-start.1
  291.7 0.0 all-reduce.3.cloned.1.call-start
  291.7 3.9 fusion.10
  295.7 4.1 fusion.11
  299.8 0.0 all-reduce.3.cloned.1.call-update
  299.8 0.3 reduce-scatter.2.cloned.1.call-start
  300.1 15.2 %all-to-all-done.1 = bf16[32,8,2048]{2,0,1:T(8,128)(2,1)S(1)} async-done(((bf16[32,8,2048]{2,0,1:T(8,128)(2,1)}), bf16[32,8,2048]{2,0,1:T(8,128)(2,1)S(1)}, u32[]{:S(2)}, u32[]{:S(2)}) %all-to-all-start.1) | async-done | bytes 1048608 | tf_op jit(solution)/shard_map/all_to_all | solution.py:61
  315.3 0.4 fusion.5
  315.7 30.1 %convolution_convert_fusion = bf16[256,16384]{1,0:T(8,128)(2,1)} fusion(bf16[256,2048]{1,0:T(8,128)(2,1)S(1)} %fusion.5, bf16[16384,2048]{1,0:T(8,128)(2,1)} %all-gather.2.cloned.1.call-done), kind=kOutput, calls=%fused_computation | convolution fusion | flops 17184063488 | bytes 76546048 | tf_op jit(solution)/shard_map/dot_general | solution.py:65
  345.8 0.0 reduce-scatter.2.cloned.1.call-update
  345.8 3.4 convolution_convert_fusion.1
  349.3 1.3 reshape.30
  350.6 29.6 %psum.22 = bf16[512]{0:T(512)(128)(2,1)S(1)} all-reduce(bf16[512]{0:T(512)(128)(2,1)S(1)} %get-tuple-element.11), channel_id=1, replica_groups=mesh['groups'=2,'tensor'=8,'dp'=2] {'tensor','dp'}, use_global_device_ids=true, to_apply=%region_3.4 | all-reduce | flops 512 | bytes 2048 | tf_op jit(solution)/shard_map/psum | solution.py:53
  380.1 0.6 convert_multiply_fusion.3
  380.7 8.9 %all-reduce.3.cloned.1.call-done = (bf16[128,512]{1,0:T(8,128)(2,1)}, bf16[512,128]{1,0:T(8,128)(2,1)}) async-done(((bf16[128,512]{1,0:T(8,128)(2,1)}, bf16[512,128]{1,0:T(8,128)(2,1)}), (bf16[128,512]{1,0:T(8,128)(2,1)}, bf16[512,128]{1,0:T(8,128)(2,1)})) %all-reduce.3.cloned.1.call-update) | async-done | bytes 262160 | tf_op jit(solution)/shard_map/psum | solution.py:52
  389.6 1.6 convert_multiply_fusion.1
  391.3 1.6 convert_multiply_fusion.2
  392.9 150.3 %reduce-scatter.2.cloned.1.call-done = bf16[256,2048]{1,0:T(8,128)(2,1)} async-done(((bf16[256,16384]{1,0:T(8,128)(2,1)}), bf16[256,2048]{1,0:T(8,128)(2,1)}) %reduce-scatter.2.cloned.1.call-update) | async-done | bytes 1048592 | tf_op jit(solution)/shard_map/reduce_scatter | solution.py:71
  543.2 3.3 fusion.8
  (36 shorter events, 0.1 us)
Async XLA Ops:
  7.2 262.0 %copy-start = (bf16[128,512]{1,0:T(8,128)(2,1)S(1)}, bf16[128,512]{1,0:T(8,128)(2,1)}, u32[]{:S(2)}) copy-start(bf16[128,512]{1,0:T(8,128)(2,1)} %param.10) | copy-start | bytes 393220
  7.2 1.3 copy-start.2
  7.2 206.8 %all-gather.2.cloned.1.call-start = ((), (), s32[]{:S(2)}) async-start(), calls=%async_computation.3 | async-start | bytes 100663296 | tf_op jit(solution)/shard_map/all_gather | solution.py:24
  8.4 29.2 %collective-permute-start = (bf16[256,2048]{1,0:T(8,128)(2,1)S(1)}, bf16[256,2048]{1,0:T(8,128)(2,1)S(1)}, u32[]{:S(2)}, u32[]{:S(2)}) collective-permute-start(bf16[256,2048]{1,0:T(8,128)(2,1)S(1)} %bitcast.61), channel_id=1, source_target_pairs={{0,2},{2,4},{4,6},{6,8},{8,10},{10,12},{12,14},{14,0},{1,3},{3,5},... | collective-permute-start | bytes 3145736 | tf_op jit(solution)/shard_map/ppermute | solution.py:16
  37.6 27.0 %collective-permute-start.1 = (bf16[256,2048]{1,0:T(8,128)(2,1)S(1)}, bf16[256,2048]{1,0:T(8,128)(2,1)S(1)}, u32[]{:S(2)}, u32[]{:S(2)}) collective-permute-start(bf16[256,2048]{1,0:T(8,128)(2,1)S(1)} %collective-permute-done), channel_id=1, source_target_pairs={{0,2},{2,4},{4,6},{6,8},{8,10},{10,12},{12,14},{14,0},{1,3},{3,5},... | collective-permute-start | bytes 3145736 | tf_op jit(solution)/shard_map/ppermute | solution.py:16
  64.6 26.1 %collective-permute-start.2 = (bf16[256,2048]{1,0:T(8,128)(2,1)S(1)}, bf16[256,2048]{1,0:T(8,128)(2,1)S(1)}, u32[]{:S(2)}, u32[]{:S(2)}) collective-permute-start(bf16[256,2048]{1,0:T(8,128)(2,1)S(1)} %collective-permute-done.1), channel_id=1, source_target_pairs={{0,2},{2,4},{4,6},{6,8},{8,10},{10,12},{12,14},{14,0},{1,3},{3,5},... | collective-permute-start | bytes 3145736 | tf_op jit(solution)/shard_map/ppermute | solution.py:16
  90.8 1.0 copy-start.4
  91.7 25.2 %collective-permute-start.3 = (bf16[256,2048]{1,0:T(8,128)(2,1)S(1)}, bf16[256,2048]{1,0:T(8,128)(2,1)S(1)}, u32[]{:S(2)}, u32[]{:S(2)}) collective-permute-start(bf16[256,2048]{1,0:T(8,128)(2,1)S(1)} %collective-permute-done.2), channel_id=1, source_target_pairs={{0,2},{2,4},{4,6},{6,8},{8,10},{10,12},{12,14},{14,0},{1,3},{3,5},... | collective-permute-start | bytes 3145736 | tf_op jit(solution)/shard_map/ppermute | solution.py:16
  116.9 1.0 copy-start.6
  117.9 24.3 %collective-permute-start.4 = (bf16[256,2048]{1,0:T(8,128)(2,1)S(1)}, bf16[256,2048]{1,0:T(8,128)(2,1)S(1)}, u32[]{:S(2)}, u32[]{:S(2)}) collective-permute-start(bf16[256,2048]{1,0:T(8,128)(2,1)S(1)} %collective-permute-done.3), channel_id=1, source_target_pairs={{0,2},{2,4},{4,6},{6,8},{8,10},{10,12},{12,14},{14,0},{1,3},{3,5},... | collective-permute-start | bytes 3145736 | tf_op jit(solution)/shard_map/ppermute | solution.py:16
  142.2 1.0 copy-start.8
  143.1 23.5 %collective-permute-start.5 = (bf16[256,2048]{1,0:T(8,128)(2,1)S(1)}, bf16[256,2048]{1,0:T(8,128)(2,1)}, u32[]{:S(2)}, u32[]{:S(2)}) collective-permute-start(bf16[256,2048]{1,0:T(8,128)(2,1)S(1)} %collective-permute-done.4), channel_id=1, source_target_pairs={{0,2},{2,4},{4,6},{6,8},{8,10},{10,12},{12,14},{14,0},{1,3},{3,5},... | collective-permute-start | bytes 3145736 | tf_op jit(solution)/shard_map/ppermute | solution.py:16
  166.6 22.8 %collective-permute-start.6 = (bf16[256,2048]{1,0:T(8,128)(2,1)}, bf16[256,2048]{1,0:T(8,128)(2,1)}, u32[]{:S(2)}, u32[]{:S(2)}) collective-permute-start(bf16[256,2048]{1,0:T(8,128)(2,1)} %collective-permute-done.5), channel_id=1, source_target_pairs={{0,2},{2,4},{4,6},{6,8},{8,10},{10,12},{12,14},{14,0},{1,3},{3,5},... | collective-permute-start | bytes 3145736 | tf_op jit(solution)/shard_map/ppermute | solution.py:16
  166.6 32.2 %copy-start.5 = (bf16[256,2048]{1,0:T(8,128)(2,1)S(1)}, bf16[256,2048]{1,0:T(8,128)(2,1)}, u32[]{:S(2)}) copy-start(bf16[256,2048]{1,0:T(8,128)(2,1)} %copy-done.4) | copy-start | bytes 3145732
  194.0 13.7 %copy-start.9 = (bf16[256,2048]{1,0:T(8,128)(2,1)S(1)}, bf16[256,2048]{1,0:T(8,128)(2,1)}, u32[]{:S(2)}) copy-start(bf16[256,2048]{1,0:T(8,128)(2,1)} %copy-done.8) | copy-start | bytes 3145732
  196.4 12.4 %copy-start.7 = (bf16[256,2048]{1,0:T(8,128)(2,1)S(1)}, bf16[256,2048]{1,0:T(8,128)(2,1)}, u32[]{:S(2)}) copy-start(bf16[256,2048]{1,0:T(8,128)(2,1)} %copy-done.6) | copy-start | bytes 3145732
  203.0 11.1 %copy-start.15 = (f32[2048]{0:T(1024)S(1)}, f32[2048]{0:T(1024)}, u32[]{:S(2)}) copy-start(f32[2048]{0:T(1024)} %param.9) | copy-start | bytes 24580
  214.0 33.4 %copy-start.11 = (bf16[1,32,16384]{2,1,0:T(8,128)(2,1)S(1)}, bf16[1,32,16384]{2,1,0:T(8,128)(2,1)}, u32[]{:S(2)}) copy-start(bf16[1,32,16384]{2,1,0:T(8,128)(2,1)} %param.13) | copy-start | bytes 3145732
  243.6 25.6 %copy-start.16 = (f32[512]{0:T(512)S(1)}, f32[512]{0:T(512)}, u32[]{:S(2)}) copy-start(f32[512]{0:T(512)} %param.11) | copy-start | bytes 6148
  243.6 23.6 %all-to-all-start = ((bf16[8,32,2048]{2,1,0:T(8,128)(2,1)}), bf16[8,32,2048]{2,1,0:T(8,128)(2,1)S(1)}, u32[]{:S(2)}, u32[]{:S(2)}) async-start(bf16[8,32,2048]{2,1,0:T(8,128)(2,1)} %bitcast.1), calls=%async_computation | async-start | bytes 2097152 | tf_op jit(solution)/shard_map/all_to_all | solution.py:30
  247.7 25.4 %copy-start.12 = (bf16[4,8,128,128]{3,2,1,0:T(8,128)(2,1)}, bf16[4,8,128,128]{3,2,1,0:T(8,128)(2,1)S(1)}, u32[]{:S(2)}) copy-start(bf16[4,8,128,128]{3,2,1,0:T(8,128)(2,1)S(1)} %copy.19) | copy-start | bytes 3145732
  269.1 3.9 copy-start.10
  269.1 3.9 copy-start.14
  276.8 2.0 copy-start.1
  284.9 10.8 %copy-start.13 = (bf16[4,8,128,128]{3,2,1,0:T(8,128)(2,1)S(1)}, bf16[4,8,128,128]{3,2,1,0:T(8,128)(2,1)}, u32[]{:S(2)}) copy-start(bf16[4,8,128,128]{3,2,1,0:T(8,128)(2,1)} %copy-done.12) | copy-start | bytes 3145732
  284.9 30.5 %copy-start.3 = (bf16[1,256,2048]{2,1,0:T(8,128)(2,1)S(1)}, bf16[1,256,2048]{2,1,0:T(8,128)(2,1)}, u32[]{:S(2)}) copy-start(bf16[1,256,2048]{2,1,0:T(8,128)(2,1)} %param.7) | copy-start | bytes 3145732
  288.1 27.2 %all-to-all-start.1 = ((bf16[32,8,2048]{2,0,1:T(8,128)(2,1)}), bf16[32,8,2048]{2,0,1:T(8,128)(2,1)S(1)}, u32[]{:S(2)}, u32[]{:S(2)}) async-start(bf16[32,8,2048]{2,0,1:T(8,128)(2,1)} %copy.14), calls=%async_computation.1 | async-start | bytes 2097152 | tf_op jit(solution)/shard_map/all_to_all | solution.py:61
  291.7 98.0 %all-reduce.3.cloned.1.call-start = ((), (), s32[]{:S(2)}) async-start(), calls=%async_computation.5 | async-start | bytes 524288 | tf_op jit(solution)/shard_map/psum | solution.py:52
  299.8 243.4 %reduce-scatter.2.cloned.1.call-start = ((), (), s32[]{:S(2)}) async-start(), calls=%async_computation.4 | async-start | bytes 9437184 | tf_op jit(solution)/shard_map/reduce_scatter | solution.py:71
Sparse Core Ops, SparseCore 0:
  9.6 97.7 all-gather.1
  299.9 89.6 all-reduce.2
  393.3 149.8 reduce-scatter.1
